TPU v7x, 32 devices: a whole 2x2x4 slice. The times are simulated.
32 devices in a mesh: groups: 2 (over x), ctx: 16 (over z, y, core).
Axes of the slice: x: 2, y: 2, z: 4, core: 2. Of those that a mesh axis runs over, the one named last changes fastest.
Arguments:
- tokens: bfloat16 [3072, 1152], P(('groups', 'ctx')), parts along dimension 0, may hold values from -100 to 100
- owner: int32 [3072, 1], P(('groups', 'ctx')), parts along dimension 0, may hold values from 0 to 15; in each aligned block of 96 rows (0 to 95, 96 to 191, ...) at most 12 rows name the same one
- slot_map: int32 [32, 16, 12], P(('groups', 'ctx')), parts along dimension 0, may hold values from 0 to 47
- sizes: int32 [3072], P(('groups', 'ctx')), parts along dimension 0, may hold values from 1 to 4
- w_query: bfloat16 [1152, 576], replicated, may hold values from -0.1875 to 0.1875
- w_key: bfloat16 [1152, 576], replicated, may hold values from -0.1875 to 0.1875
- w_value: bfloat16 [1152, 576], replicated, may hold values from -0.1875 to 0.1875
- w_out: bfloat16 [576, 1152], replicated, may hold values from -0.25 to 0.25
Outputs:
- mixed: bfloat16 [3072, 1152], P(('groups', 'ctx')), parts along dimension 0
There are 2 independent parts, one for each index of `groups`. A program takes and returns all parts, laid end to end along the dimension named above; an argument that names none is the same for every part. Nothing has to cross between parts.
Inputs may be any that keep to these rules, and one draw needn't show every extreme that they name: Among the source tokens of one index of ctx, at most 12 name the same owner, and in some index exactly 12 do.
All inputs are finite; a program needn't handle non-finite values.
Results may differ from a plain program's by a relative error of at most 0.0085.
The roundings to bfloat16 on the way count: a program that leaves them out, or rounds other values in their place, can miss the bound.
Values may be sent and summed in bfloat16 or wider, within the bound.
A program may use at most 128 MiB of HBM per device.

v0:
```python
import math
import jax
import jax.numpy as jnp
from jax import lax
from jax.sharding import PartitionSpec as P

HEADS = 8
HEAD = 72


def on_device(tokens, owner, slot_map, sizes, w_query, w_key, w_value, w_out):
    tok_rows = tokens.shape[0]
    shards = lax.axis_size("ctx")
    slots = slot_map.shape[2]
    places = shards * slots
    merged_rows = tok_rows // 2
    owners = owner[:, 0]
    marks = (owners[:, None] == jnp.arange(shards, dtype=jnp.int32)[None, :]).astype(jnp.int32)
    ranking = jnp.sum((jnp.cumsum(marks, axis=0) - marks) * marks, axis=1)
    bucket = owners * slots + ranking
    to_bucket = (bucket[:, None] == jnp.arange(places, dtype=jnp.int32)[None, :]).astype(
        jnp.bfloat16
    )
    outgoing = jnp.einsum(
        "tp,td->pd", to_bucket, tokens, preferred_element_type=jnp.float32
    ).astype(jnp.bfloat16)
    out_weights = jnp.einsum(
        "tp,t->p", to_bucket, sizes.astype(jnp.bfloat16), preferred_element_type=jnp.float32
    ).astype(jnp.bfloat16)
    received, in_weights = (
        lax.all_to_all(
            outgoing.reshape(shards, slots, -1), "ctx", split_axis=0, concat_axis=0, tiled=True
        ),
        lax.all_to_all(
            out_weights.reshape(shards, slots), "ctx", split_axis=0, concat_axis=0, tiled=True
        ),
    )
    targets = slot_map[0].reshape(places)
    landing = targets[None, :] == jnp.arange(merged_rows, dtype=jnp.int32)[:, None]
    weighted = jnp.where(landing, in_weights.reshape(places)[None, :], 0)
    merged_sum = jnp.dot(weighted, received.reshape(places, -1), preferred_element_type=jnp.float32)
    counts = jnp.sum(weighted.astype(jnp.float32), axis=1)
    merged = (merged_sum / jnp.maximum(counts, 1.0)[:, None]).astype(jnp.bfloat16)
    key_bias = jnp.where(counts > 0, jnp.log(jnp.maximum(counts, 1.0)), -1e30).astype(jnp.bfloat16)
    queries = jnp.dot(merged, w_query, preferred_element_type=jnp.float32).astype(jnp.bfloat16)
    query_heads = queries.reshape(merged_rows, HEADS, HEAD)
    inverse = 1.0 / math.sqrt(HEAD)

    def attend_block(carry, item):
        row_max, total, accum = carry
        key_heads, value_heads, bias = item
        scores = (
            jnp.einsum("qhd,khd->hqk", query_heads, key_heads, preferred_element_type=jnp.float32)
            * inverse
        )
        scores = scores + bias.astype(jnp.float32)[None, None, :]
        new_max = jnp.maximum(row_max, jnp.max(scores, axis=2))
        factor = jnp.exp(row_max - new_max)
        expo = jnp.exp(scores - new_max[:, :, None])
        total = total * factor + jnp.sum(expo, axis=2)
        accum = accum * factor[:, :, None] + jnp.einsum(
            "hqk,khd->hqd",
            expo.astype(jnp.bfloat16),
            value_heads,
            preferred_element_type=jnp.float32,
        )
        return ((new_max, total, accum), None)

    start_state = (
        jnp.full((HEADS, merged_rows), -jnp.inf, jnp.float32),
        jnp.zeros((HEADS, merged_rows), jnp.float32),
        jnp.zeros((HEADS, merged_rows, HEAD), jnp.float32),
    )
    own_keys = jnp.dot(merged, w_key, preferred_element_type=jnp.float32).astype(jnp.bfloat16)
    own_values = jnp.dot(merged, w_value, preferred_element_type=jnp.float32).astype(jnp.bfloat16)
    carry = start_state
    keys = lax.all_gather(own_keys, "ctx", axis=0, tiled=True)
    values = lax.all_gather(own_values, "ctx", axis=0, tiled=True)
    bias = lax.all_gather(key_bias, "ctx", axis=0, tiled=True)
    length = keys.shape[0]
    block = math.gcd(length, 1536)
    turns = length // block
    items = (
        keys.reshape(turns, block, HEADS, HEAD),
        values.reshape(turns, block, HEADS, HEAD),
        bias.reshape(turns, block),
    )
    carry, unused = lax.scan(attend_block, carry, items)
    row_max, total, accum = carry
    attended = (
        jnp.transpose(accum / total[:, :, None], (1, 0, 2))
        .reshape(merged_rows, HEADS * HEAD)
        .astype(jnp.bfloat16)
    )
    landing_rows = landing.astype(jnp.bfloat16)
    leaving = jnp.einsum(
        "mp,md->pd", landing_rows, attended, preferred_element_type=jnp.float32
    ).astype(jnp.bfloat16)
    returned = lax.all_to_all(
        leaving.reshape(shards, slots, -1), "ctx", split_axis=0, concat_axis=0, tiled=True
    )
    picked = jnp.einsum(
        "tp,pd->td", to_bucket, returned.reshape(places, -1), preferred_element_type=jnp.float32
    ).astype(jnp.bfloat16)
    mixed = jnp.dot(picked, w_out, preferred_element_type=jnp.float32).astype(jnp.bfloat16)
    return mixed


def solution(mesh):
    in_specs = (
        P(("groups", "ctx"), None),
        P(("groups", "ctx"), None),
        P(("groups", "ctx"), None, None),
        P(("groups", "ctx")),
        P(),
        P(),
        P(),
        P(),
    )
    out_specs = P(("groups", "ctx"), None)
    return jax.shard_map(
        on_device, mesh=mesh, in_specs=in_specs, out_specs=out_specs, check_vma=False
    )
```

profile of v0, /device:TPU:0, one launch (start us, length us, event | category | flops | bytes accessed | tf_op | source)
XLA Modules:
  0.0 126.5 jit_solution(1130961317788527914)
XLA Ops:
  0.0 0.0 copy-start
  0.0 0.8 fusion.16
  0.8 0.1 reduce_window_sum.11
  1.0 0.8 select_reduce_fusion
  1.8 0.7 fusion.23
  2.5 0.8 fusion.10
  3.3 0.7 all_to_all.16
  4.1 7.4 %all-to-all-start = ((bf16[16,1,12]{2,1,0:T(2,128)(2,1)}), bf16[16,1,12]{2,1,0:T(2,128)(2,1)S(1)}, u32[]{:S(2)}, u32[]{:S(2)}) async-start(bf16[16,1,12]{2,1,0:T(2,128)(2,1)} %all_to_all.16), calls=%async_computation | async-start | bytes 16384 | tf_op jit(solution)/shard_map/all_to_all | solution.py:34
  11.5 0.0 copy-start.3
  11.5 0.0 copy-start.4
  11.5 1.3 %convolution_convert_fusion = bf16[192,1152]{1,0:T(8,128)(2,1)S(1)} fusion(bf16[96,1152]{1,0:T(8,128)(2,1)} %param.8, s32[96]{0:T(128)S(1)} %fusion.23), kind=kOutput, calls=%fused_computation | convolution fusion | flops 42706944 | bytes 663936 | tf_op jit(solution)/shard_map/tp,td->pd/dot_general | solution.py:24
  12.8 0.9 reshape.49
  13.8 4.1 %all-to-all-done = bf16[16,1,12]{2,1,0:T(2,128)(2,1)S(1)} async-done(((bf16[16,1,12]{2,1,0:T(2,128)(2,1)}), bf16[16,1,12]{2,1,0:T(2,128)(2,1)S(1)}, u32[]{:S(2)}, u32[]{:S(2)}) %all-to-all-start) | async-done | bytes 416 | tf_op jit(solution)/shard_map/all_to_all | solution.py:34
  17.8 3.6 %all-to-all-start.1 = ((bf16[16,12,1152]{2,1,0:T(8,128)(2,1)}), bf16[16,12,1152]{2,1,0:T(8,128)(2,1)S(1)}, u32[]{:S(2)}, u32[]{:S(2)}) async-start(bf16[16,12,1152]{2,1,0:T(8,128)(2,1)} %reshape.49), calls=%async_computation.1 | async-start | bytes 1179648 | tf_op jit(solution)/shard_map/all_to_all | solution.py:31
  21.4 0.0 copy-start.1
  21.4 0.0 copy-done.3
  21.5 0.1 copy.23
  21.5 0.1 eq.53
  21.6 0.0 copy-done.4
  21.6 0.6 dynamic-slice.1
  22.9 0.1 broadcast_in_dim.39
  23.0 0.1 convert_reduce_fusion
  23.2 0.2 dynamic-update-slice
  23.4 35.8 %all-reduce = bf16[768]{0:T(1024)(128)(2,1)S(1)} all-reduce(bf16[768]{0:T(1024)(128)(2,1)S(1)} %dynamic-update-slice), channel_id=1, replica_groups=mesh['groups'=2,'ctx'=16] {'ctx'}, use_global_device_ids=true, to_apply=%add | all-reduce | flops 768 | bytes 3072
  59.2 0.0 all-to-all-done.1
  59.2 0.9 reshape.50
  60.1 1.2 fusion
  61.3 0.0 copy-done.1
  61.3 0.5 convolution_convert_fusion.4
  61.8 20.4 %all_gather.11 = bf16[768,576]{1,0:T(8,128)(2,1)S(1)} all-gather(bf16[48,576]{1,0:T(8,128)(2,1)S(1)} %convolution_convert_fusion.4), channel_id=1, replica_groups=mesh['groups'=2,'ctx'=16] {'ctx'}, dimensions={0}, use_global_device_ids=true | all-gather | bytes 940032 | tf_op jit(solution)/shard_map/all_gather | solution.py:78
  82.2 1.3 %copy.27 = bf16[768,576]{0,1:T(8,128)(2,1)} copy(bf16[768,576]{1,0:T(8,128)(2,1)S(1)} %all_gather.11) | data formatting | bytes 1769472 | tf_op jit(solution)/shard_map/all_gather | solution.py:78
  83.4 1.8 %convolution_convert_fusion.5 = bf16[48,576]{1,0:T(8,128)(2,1)S(1)} fusion(bf16[48,1152]{1,0:T(8,128)(2,1)S(1)} %fusion, bf16[1152,576]{0,1:T(8,128)(2,1)} %param.13), kind=kOutput, calls=%fused_computation.14 | convolution fusion | flops 63728640 | bytes 1492992 | tf_op jit(solution)/shard_map/dot_general | solution.py:74
  85.2 21.5 %all_gather.9 = bf16[768,576]{1,0:T(8,128)(2,1)S(1)} all-gather(bf16[48,576]{1,0:T(8,128)(2,1)S(1)} %convolution_convert_fusion.5), channel_id=1, replica_groups=mesh['groups'=2,'ctx'=16] {'ctx'}, dimensions={0}, use_global_device_ids=true | all-gather | bytes 940032 | tf_op jit(solution)/shard_map/all_gather | solution.py:77
  106.8 0.6 copy.25
  107.4 1.8 %convolution_convert_fusion.6 = bf16[48,576]{1,0:T(8,128)(2,1)S(1)} fusion(bf16[48,1152]{1,0:T(8,128)(2,1)S(1)} %fusion, bf16[1152,576]{0,1:T(8,128)(2,1)} %param.12), kind=kOutput, calls=%fused_computation.15 | convolution fusion | flops 63728640 | bytes 1492992 | tf_op jit(solution)/shard_map/dot_general | solution.py:45
  109.2 0.1 reshape.51
  109.3 0.0 copy-start.2
  109.3 0.4 fusion.25
  109.7 0.4 fusion.5
  110.1 0.4 copy-done.2
  110.5 0.4 fusion.4
  111.0 0.1 convert_element_type.72
  111.1 0.3 convolution_convert_fusion.2
  111.4 0.1 reshape.52
  111.4 13.7 %all_to_all.20 = bf16[16,12,576]{2,1,0:T(8,128)(2,1)S(1)} all-to-all(bf16[16,12,576]{2,1,0:T(8,128)(2,1)S(1)} %reshape.52), channel_id=1, replica_groups=mesh['groups'=2,'ctx'=16] {'ctx'}, dimensions={0} | all-to-all | bytes 442368 | tf_op jit(solution)/shard_map/all_to_all | solution.py:99
  125.1 0.1 reshape.53
  125.2 0.0 copy-done
  125.2 1.2 convolution_convert_fusion.1
  (8 shorter events, 0.1 us)
Async XLA Ops:
  0.0 125.2 %copy-start = (bf16[576,1152]{1,0:T(8,128)(2,1)S(1)}, bf16[576,1152]{1,0:T(8,128)(2,1)}, u32[]{:S(2)}) copy-start(bf16[576,1152]{1,0:T(8,128)(2,1)} %param.15) | copy-start | bytes 3981316
  4.1 13.8 %all-to-all-start = ((bf16[16,1,12]{2,1,0:T(2,128)(2,1)}), bf16[16,1,12]{2,1,0:T(2,128)(2,1)S(1)}, u32[]{:S(2)}, u32[]{:S(2)}) async-start(bf16[16,1,12]{2,1,0:T(2,128)(2,1)} %all_to_all.16), calls=%async_computation | async-start | bytes 16384 | tf_op jit(solution)/shard_map/all_to_all | solution.py:34
  11.5 10.0 %copy-start.3 = (s32[1,16,12]{1,0,2:T(1,128)S(1)}, s32[1,16,12]{1,0,2:T(1,128)}, u32[]{:S(2)}) copy-start(s32[1,16,12]{1,0,2:T(1,128)} %param.10) | copy-start | bytes 2308
  11.5 10.1 %copy-start.4 = (u32[32]{0:T(128)S(1)}, u32[32]{0:T(128)}, u32[]{:S(2)}) copy-start(u32[32]{0:T(128)} %constant.40) | copy-start | bytes 388
  17.8 41.4 %all-to-all-start.1 = ((bf16[16,12,1152]{2,1,0:T(8,128)(2,1)}), bf16[16,12,1152]{2,1,0:T(8,128)(2,1)S(1)}, u32[]{:S(2)}, u32[]{:S(2)}) async-start(bf16[16,12,1152]{2,1,0:T(8,128)(2,1)} %reshape.49), calls=%async_computation.1 | async-start | bytes 1179648 | tf_op jit(solution)/shard_map/all_to_all | solution.py:31
  21.4 39.9 %copy-start.1 = (bf16[1152,576]{0,1:T(8,128)(2,1)S(1)}, bf16[1152,576]{0,1:T(8,128)(2,1)}, u32[]{:S(2)}) copy-start(bf16[1152,576]{0,1:T(8,128)(2,1)} %param.14) | copy-start | bytes 3981316
  109.3 1.2 copy-start.2
where the time goes:
time: 127 us; the launch traced here: 126 us
  blocking collectives  91.4 us (72%)
  starting transfers between devices  11 us (9%)
  matrix products  9.81 us (8%)
  local copies, waits for them, and re-layouts  6.33 us (5%)
  waiting for transfers between devices  4.09 us (3%)
  other arithmetic  3.01 us (2%)
    unnamed x1, blocking collectives  35.8 us
    all_gather x1, blocking collectives, on_device(): keys = lax.all_gather(own_keys, 'ctx', axis=0, tiled=True)  21.5 us
    all_gather x1, blocking collectives, on_device(): values = lax.all_gather(own_values, 'ctx', axis=0, tiled=True)  20.4 us
    all_to_all x1, blocking collectives, on_device(): lax.all_to_all(leaving.reshape(shards, slots, -1), 'ctx', split_axis=0, c...  13.7 us
    all_to_all x1, starting transfers between devices, on_device(): lax.all_to_all(out_weights.reshape(shards, slots), 'ctx', split_axis=0, c...  7.41 us
    all_to_all x1, waiting for transfers between devices, on_device(): lax.all_to_all(out_weights.reshape(shards, slots), 'ctx', split_axis=0, c...  4.09 us
    all_to_all x1, starting transfers between devices, on_device(): lax.all_to_all(outgoing.reshape(shards, slots, -1), 'ctx', split_axis=0,...  3.58 us
  transfers between devices with their start and end apart: 2, of which 1 were waited for; matrix products, arithmetic and copies ran while one was open for 3% of the time, Pallas kernels for 0%

commit v1 on v0

--- a/solution.py
+++ b/solution.py
@@ -74,8 +74,9 @@
     own_keys = jnp.dot(merged, w_key, preferred_element_type=jnp.float32).astype(jnp.bfloat16)
     own_values = jnp.dot(merged, w_value, preferred_element_type=jnp.float32).astype(jnp.bfloat16)
     carry = start_state
-    keys = lax.all_gather(own_keys, "ctx", axis=0, tiled=True)
-    values = lax.all_gather(own_values, "ctx", axis=0, tiled=True)
+    frame_out = jnp.concatenate([own_keys, own_values], axis=1)
+    earlier = jax.lax.all_gather(frame_out, axis_name="ctx", axis=0, tiled=True)
+    keys, values = jnp.split(earlier, [own_keys.shape[1]], axis=1)
     bias = lax.all_gather(key_bias, "ctx", axis=0, tiled=True)
     length = keys.shape[0]
     block = math.gcd(length, 1536)

time: 127 us -> 119 us (0.937)
  blocking collectives: 91.4 us -> 47.1 us
  waiting for transfers between devices: 4.09 us -> 23.8 us
  between operations: 0.88 us -> 14.3 us
  local copies, waits for them, and re-layouts: 6.33 us -> 9.3 us
    all_gather x2 -> x0, blocking collectives: 41.9 us -> none  [the longest x1 21.5 us: on_device(): keys = lax.all_gather(own_keys, 'ctx', axis=0, tiled=True)]
    all_to_all x1, waiting for transfers between devices: 0.01 us -> 15 us  [on_device(): lax.all_to_all(outgoing.reshape(shards, slots, -1), 'ctx', split_axis=0,...]
    all_gather x0 -> x1, waiting for transfers between devices: none -> 4.67 us  [on_device(): earlier = jax.lax.all_gather(frame_out, axis_name='ctx', axis=0, tiled=True)]
    split x0 -> x3, local copies, waits for them, and re-layouts: none -> 4.56 us  [on_device(): keys, values = jnp.split(earlier, [own_keys.shape[1]], axis=1)]
    unnamed x1, blocking collectives: 35.8 us -> 32.6 us
    all_gather x2 -> x0, local copies, waits for them, and re-layouts: 1.88 us -> none  [the longest x1 1.29 us: on_device(): values = lax.all_gather(own_values, 'ctx', axis=0, tiled=True)]
    dot_general x1, matrix products: 1.8 us -> 0.47 us  [on_device(): jnp.dot(merged, w_query, preferred_element_type=jnp.float32)]
    dot_general x1, matrix products: 1.79 us -> 0.47 us  [on_device(): jnp.dot(merged, w_key, preferred_element_type=jnp.float32)]
  transfers between devices with their start and end apart: 2 -> 3, of which waited for: 1 -> 3; matrix products, arithmetic and copies ran while one was open for 3% -> 4% of each run, Pallas kernels for 0% -> 0%
where the time goes in v1:
time: 119 us
  blocking collectives  47.1 us (40%)
  waiting for transfers between devices  23.8 us (20%)
  between operations  14.3 us (12%)
  starting transfers between devices  11 us (9%)
  matrix products  9.66 us (8%)
  local copies, waits for them, and re-layouts  9.3 us (8%)
  other arithmetic  3.73 us (3%)
    unnamed x1, blocking collectives  32.6 us
    all_to_all x1, waiting for transfers between devices, on_device(): lax.all_to_all(outgoing.reshape(shards, slots, -1), 'ctx', split_axis=0,...  15 us
    all_to_all x1, blocking collectives, on_device(): lax.all_to_all(leaving.reshape(shards, slots, -1), 'ctx', split_axis=0, c...  14.5 us
    all_to_all x1, starting transfers between devices, on_device(): lax.all_to_all(out_weights.reshape(shards, slots), 'ctx', split_axis=0, c...  7.41 us
    all_gather x1, waiting for transfers between devices, on_device(): earlier = jax.lax.all_gather(frame_out, axis_name='ctx', axis=0, tiled=True)  4.67 us
    split x3, local copies, waits for them, and re-layouts, on_device(): keys, values = jnp.split(earlier, [own_keys.shape[1]], axis=1)  4.56 us
    all_to_all x1, waiting for transfers between devices, on_device(): lax.all_to_all(out_weights.reshape(shards, slots), 'ctx', split_axis=0, c...  4.1 us
    all_to_all x1, starting transfers between devices, on_device(): lax.all_to_all(outgoing.reshape(shards, slots, -1), 'ctx', split_axis=0,...  3.58 us
  transfers between devices with their start and end apart: 3, of which 3 were waited for; matrix products, arithmetic and copies ran while one was open for 4% of the time, Pallas kernels for 0%

profile of v1, /device:TPU:0, one launch (start us, length us, event | category | flops | bytes accessed | tf_op | source)
XLA Modules:
  0.0 118.9 jit_solution(1695023652842360894)
XLA Ops:
  6.5 0.0 copy-start
  6.5 0.8 fusion.16
  7.4 0.1 reduce_window_sum.11
  7.5 0.8 select_reduce_fusion
  8.4 0.7 fusion.23
  9.0 0.8 fusion.10
  9.9 0.7 all_to_all.16
  10.6 7.4 %all-to-all-start = ((bf16[16,1,12]{2,1,0:T(2,128)(2,1)}), bf16[16,1,12]{2,1,0:T(2,128)(2,1)S(1)}, u32[]{:S(2)}, u32[]{:S(2)}) async-start(bf16[16,1,12]{2,1,0:T(2,128)(2,1)} %all_to_all.16), calls=%async_computation | async-start | bytes 16384 | tf_op jit(solution)/shard_map/all_to_all | solution.py:34
  18.0 0.0 copy-start.4
  18.0 1.3 %convolution_convert_fusion = bf16[192,1152]{1,0:T(8,128)(2,1)S(1)} fusion(bf16[96,1152]{1,0:T(8,128)(2,1)} %param.8, s32[96]{0:T(128)S(1)} %fusion.23), kind=kOutput, calls=%fused_computation | convolution fusion | flops 42706944 | bytes 663936 | tf_op jit(solution)/shard_map/tp,td->pd/dot_general | solution.py:24
  19.4 0.9 reshape.49
  20.3 4.1 %all-to-all-done = bf16[16,1,12]{2,1,0:T(2,128)(2,1)S(1)} async-done(((bf16[16,1,12]{2,1,0:T(2,128)(2,1)}), bf16[16,1,12]{2,1,0:T(2,128)(2,1)S(1)}, u32[]{:S(2)}, u32[]{:S(2)}) %all-to-all-start) | async-done | bytes 416 | tf_op jit(solution)/shard_map/all_to_all | solution.py:34
  24.4 3.6 %all-to-all-start.1 = ((bf16[16,12,1152]{2,1,0:T(8,128)(2,1)}), bf16[16,12,1152]{2,1,0:T(8,128)(2,1)S(1)}, u32[]{:S(2)}, u32[]{:S(2)}) async-start(bf16[16,12,1152]{2,1,0:T(8,128)(2,1)} %reshape.49), calls=%async_computation.1 | async-start | bytes 1179648 | tf_op jit(solution)/shard_map/all_to_all | solution.py:31
  28.0 0.0 copy-start.1
  28.0 0.0 all-gather.2.cloned.1.call-start
  28.0 0.0 copy-done.4
  28.0 0.1 copy.23
  28.1 0.1 eq.53
  28.2 0.1 broadcast_in_dim.39
  28.3 0.1 convert_reduce_fusion
  28.5 15.0 %all-to-all-done.1 = bf16[16,12,1152]{2,1,0:T(8,128)(2,1)S(1)} async-done(((bf16[16,12,1152]{2,1,0:T(8,128)(2,1)}), bf16[16,12,1152]{2,1,0:T(8,128)(2,1)S(1)}, u32[]{:S(2)}, u32[]{:S(2)}) %all-to-all-start.1) | async-done | bytes 442400 | tf_op jit(solution)/shard_map/all_to_all | solution.py:31
  43.4 0.9 reshape.50
  44.3 0.0 copy-start.2
  44.3 1.3 %fusion = bf16[48,1152]{1,0:T(8,128)(2,1)S(1)} fusion(bf16[192,1152]{1,0:T(8,128)(2,1)} %reshape.50, f32[48]{0:T(128)S(1)} %get-tuple-element.22, s32[192]{0:T(256)S(1)} %eq.53, bf16[192]{0:T(256)(128)(2,1)S(1)} %broadcast_in_dim.39), kind=kOutput, calls=%fused_computation.3 | convolution fusion | flops 21362688 | bytes 554304 | tf_op jit(solution)/shard_map/dot_general | solution.py:41
  45.6 0.0 copy-done.1
  45.6 0.0 copy-start.5
  45.7 0.5 convolution_convert_fusion.4
  46.1 0.0 copy-done.2
  46.1 0.0 copy-start.3
  46.2 0.5 convolution_convert_fusion.5
  46.6 0.7 pad_maximum_fusion
  47.4 0.0 all-gather.2.cloned.1.call-update
  47.4 0.0 copy-done.5
  47.4 0.6 dynamic-slice.1
  48.7 0.2 dynamic-update-slice
  48.9 32.6 %all-reduce = bf16[768]{0:T(1024)(128)(2,1)S(1)} all-reduce(bf16[768]{0:T(1024)(128)(2,1)S(1)} %dynamic-update-slice), channel_id=1, replica_groups=mesh['groups'=2,'ctx'=16] {'ctx'}, use_global_device_ids=true, to_apply=%add | all-reduce | flops 768 | bytes 3072
  81.5 0.0 copy-done.3
  81.5 0.5 convolution_convert_fusion.6
  82.0 0.8 reshape.51
  82.8 4.7 %all-gather.2.cloned.1.call-done = bf16[768,1152]{1,0:T(8,128)(2,1)} async-done(((bf16[48,1152]{1,0:T(8,128)(2,1)}), bf16[768,1152]{1,0:T(8,128)(2,1)}) %all-gather.2.cloned.1.call-update) | async-done | bytes 1769488 | tf_op jit(solution)/shard_map/all_gather | solution.py:78
  87.4 2.0 %fusion.25 = (bf16[768,576]{1,0:T(8,128)(2,1)S(1)}, bf16[768,576]{1,0:T(8,128)(2,1)S(1)}) fusion(bf16[768,1152]{1,0:T(8,128)(2,1)} %all-gather.2.cloned.1.call-done), kind=kLoop, calls=%fused_computation.45 | loop fusion | bytes 3538944 | tf_op jit(solution)/shard_map/split | solution.py:79
  89.4 1.3 %copy.25 = bf16[768,576]{0,1:T(8,128)(2,1)} copy(bf16[768,576]{1,0:T(8,128)(2,1)S(1)} %get-tuple-element.19) | data formatting | bytes 1769472 | tf_op jit(solution)/shard_map/split | solution.py:79
  90.7 1.6 %fusion.26 = (f32[8,48]{1,0:T(8,128)S(1)}, f32[8,48,768]{2,1,0:T(8,128)S(1)}) fusion(f32[768]{0:T(1024)S(1)} %convert_element_type.69, bf16[768,8,72]{0,2,1:T(8,128)(2,1)} %bitcast.41, bf16[48,8,72]{2,1,0:T(8,128)(2,1)} %reshape.51), kind=kOutput, calls=%fused_computation.46 | convolution fusion | flops 43351680 | bytes 2124288 | tf_op jit(solution)/shard_map/while/body/eval_jaxpr/qhd,khd->hqk/dot_general | solution.py:53
  92.3 0.3 fusion.5
  92.7 1.3 %copy.27 = bf16[768,576]{0,1:T(8,128)(2,1)} copy(bf16[768,576]{1,0:T(8,128)(2,1)S(1)} %get-tuple-element.20) | data formatting | bytes 1769472 | tf_op jit(solution)/shard_map/split | solution.py:79
  94.0 1.6 %fusion.4 = bf16[48,8,72]{2,0,1:T(8,128)(2,1)S(1)} fusion(bf16[768,8,72]{0,2,1:T(8,128)(2,1)} %bitcast.42, f32[8,48,768]{2,1,0:T(8,128)S(1)} %get-tuple-element.32, f32[8,48]{1,0:T(8,128)S(1)} %get-tuple-element.23, f32[48,8]{0,1:T(8,128)S(1)} %bitcast_add_fusion, f32[48,8]{0,1:T(8,128)S(1)} %multiply_bitcast_fusion), kind=kOutput, calls=%fused_computation.12 | convolution fusion | flops 43140096 | bytes 2124288 | tf_op jit(solution)/shard_map/while/body/eval_jaxpr/hqk,khd->hqd/dot_general | solution.py:61
  95.6 0.1 convert_element_type.72
  95.8 0.3 convolution_convert_fusion.2
  96.1 0.1 reshape.52
  96.1 14.5 %all_to_all.20 = bf16[16,12,576]{2,1,0:T(8,128)(2,1)S(1)} all-to-all(bf16[16,12,576]{2,1,0:T(8,128)(2,1)S(1)} %reshape.52), channel_id=1, replica_groups=mesh['groups'=2,'ctx'=16] {'ctx'}, dimensions={0} | all-to-all | bytes 442368 | tf_op jit(solution)/shard_map/all_to_all | solution.py:100
  110.7 0.1 reshape.53
  110.8 0.0 copy-done
  110.8 1.2 %convolution_convert_fusion.1 = bf16[96,1152]{1,0:T(8,128)(2,1)} fusion(bf16[576,1152]{1,0:T(8,128)(2,1)S(1)} %copy-done, bf16[192,576]{1,0:T(8,128)(2,1)S(1)} %reshape.53, s32[96]{0:T(128)S(1)} %fusion.23), kind=kOutput, calls=%fused_computation.1 | convolution fusion | flops 148819968 | bytes 1769856 | tf_op jit(solution)/shard_map/dot_general | solution.py:106
  (8 shorter events, 0.1 us)
Async XLA Ops:
  6.5 104.2 %copy-start = (bf16[576,1152]{1,0:T(8,128)(2,1)S(1)}, bf16[576,1152]{1,0:T(8,128)(2,1)}, u32[]{:S(2)}) copy-start(bf16[576,1152]{1,0:T(8,128)(2,1)} %param.15) | copy-start | bytes 3981316
  10.6 13.8 %all-to-all-start = ((bf16[16,1,12]{2,1,0:T(2,128)(2,1)}), bf16[16,1,12]{2,1,0:T(2,128)(2,1)S(1)}, u32[]{:S(2)}, u32[]{:S(2)}) async-start(bf16[16,1,12]{2,1,0:T(2,128)(2,1)} %all_to_all.16), calls=%async_computation | async-start | bytes 16384 | tf_op jit(solution)/shard_map/all_to_all | solution.py:34
  18.0 10.0 %copy-start.4 = (s32[1,16,12]{1,0,2:T(1,128)S(1)}, s32[1,16,12]{1,0,2:T(1,128)}, u32[]{:S(2)}) copy-start(s32[1,16,12]{1,0,2:T(1,128)} %param.10) | copy-start | bytes 2308
  24.4 19.1 %all-to-all-start.1 = ((bf16[16,12,1152]{2,1,0:T(8,128)(2,1)}), bf16[16,12,1152]{2,1,0:T(8,128)(2,1)S(1)}, u32[]{:S(2)}, u32[]{:S(2)}) async-start(bf16[16,12,1152]{2,1,0:T(8,128)(2,1)} %reshape.49), calls=%async_computation.1 | async-start | bytes 1179648 | tf_op jit(solution)/shard_map/all_to_all | solution.py:31
  28.0 17.7 %copy-start.1 = (bf16[1152,576]{0,1:T(8,128)(2,1)S(1)}, bf16[1152,576]{0,1:T(8,128)(2,1)}, u32[]{:S(2)}) copy-start(bf16[1152,576]{0,1:T(8,128)(2,1)} %param.14) | copy-start | bytes 3981316
  28.0 59.5 %all-gather.2.cloned.1.call-start = ((), (), s32[]{:S(2)}) async-start(), calls=%async_computation.3 | async-start | bytes 1880064 | tf_op jit(solution)/shard_map/all_gather | solution.py:78
  44.3 1.8 %copy-start.2 = (bf16[1152,576]{0,1:T(8,128)(2,1)S(1)}, bf16[1152,576]{0,1:T(8,128)(2,1)}, u32[]{:S(2)}) copy-start(bf16[1152,576]{0,1:T(8,128)(2,1)} %param.13) | copy-start | bytes 3981316
  45.6 1.8 %copy-start.5 = (u32[32]{0:T(128)S(1)}, u32[32]{0:T(128)}, u32[]{:S(2)}) copy-start(u32[32]{0:T(128)} %constant.40) | copy-start | bytes 388
  46.1 35.4 %copy-start.3 = (bf16[1152,576]{0,1:T(8,128)(2,1)S(1)}, bf16[1152,576]{0,1:T(8,128)(2,1)}, u32[]{:S(2)}) copy-start(bf16[1152,576]{0,1:T(8,128)(2,1)} %param.12) | copy-start | bytes 3981316
Sparse Core Ops, SparseCore 0:
  47.5 39.8 all-gather.1
